TPU v7x, 32 devices: a whole 2x2x4 slice. The times are simulated.
32 devices in a mesh: mode: 4 (over y, x), rest: 8 (over z, core).
Axes of the slice: x: 2, y: 2, z: 4, core: 2. Of those that a mesh axis runs over, the one named last changes fastest.
Arguments:
- unfolded: float32 [512, 65536], P('mode', 'rest'), may hold values from -150 to 150
- start_block: float32 [512, 128], replicated, may hold values from -6 to 6
Outputs:
- triangle: float32 [512, 512], replicated
- factor: float32 [512, 128], replicated
- core: float32 [128, 65536], P('mode', 'rest')
All inputs are finite; a program needn't handle non-finite values.
Results may differ from a plain program's by a relative error of at most 0.0003.
Values sent between devices are 32-bit elements; how exact they have to be, the bound alone decides.
A program may use at most 64 MiB of HBM per device.

v0:
```python
import functools

import jax
import jax.numpy as jnp
from jax import lax
from jax.experimental import pallas as pl
from jax.experimental.pallas import tpu as pltpu
from jax.sharding import PartitionSpec as P

ITERS = 3
SUB = 8
LANES = 128
F32 = jnp.float32
BF16 = jnp.bfloat16


def parts3(x):
    hi = x.astype(BF16).astype(F32)
    rest = x - hi
    mid = rest.astype(BF16).astype(F32)
    return hi, mid, rest - mid


def dot3(x, y, dims):
    xh = x.astype(BF16)
    xl = (x - xh.astype(F32)).astype(BF16)
    yh = y.astype(BF16)
    yl = (y - yh.astype(F32)).astype(BF16)
    dot = functools.partial(lax.dot_general, dimension_numbers=(dims, ((), ())), preferred_element_type=F32)
    return dot(xh, yh) + (dot(xh, yl) + dot(xl, yh))


def dotf(x, y, dims):
    return lax.dot_general(
        x, y, (dims, ((), ())), precision=lax.Precision.HIGHEST, preferred_element_type=F32
    )


def eliminate(ref, row, col, width, block):
    r0 = pl.multiple_of(block * SUB, SUB)
    v = ref[pl.ds(row + r0, SUB), pl.ds(col, width)]
    sub = lax.broadcasted_iota(jnp.int32, (SUB, 1), 0)
    d = pltpu.roll(v[:, :LANES], lax.rem(LANES - r0, LANES), 1)
    pivots = jnp.ones((SUB, 1), F32)
    for k in range(SUB):
        c = d[:, k : k + 1]
        p = c[k : k + 1, :]
        f = jnp.where(sub > k, c / p, 0.0)
        pivots = jnp.where(sub == k, p, pivots)
        if k < SUB - 1:
            d = d - f * d[k : k + 1, :]
            v = v - f * v[k : k + 1, :]
    s = lax.rsqrt(pivots)
    s = s * (1.5 - 0.5 * pivots * s * s)
    v = v * s
    ref[pl.ds(row + r0, SUB), pl.ds(col, width)] = v
    lane = lax.broadcasted_iota(jnp.int32, (SUB, LANES), 1)
    keep = lane >= r0 + SUB
    hi, mid, lo = parts3(v)
    lh, lm, ll = (jnp.where(keep, x[:, :LANES], 0.0) for x in (hi, mid, lo))
    left = jnp.concatenate([lh, lh, lm, lm, lh, ll], axis=0).astype(BF16)
    right = jnp.concatenate([hi, mid, hi, mid, lo, hi], axis=0).astype(BF16)
    upd = lax.dot_general(left, right, (((0,), (0,)), ((), ())), preferred_element_type=F32)
    ref[pl.ds(row, LANES), pl.ds(col, width)] -= upd


def solve_kernel(gram_ref, start_ref, tri_ref, factor_ref, basis_ref, work, aug):
    m = gram_ref.shape[0]
    r = start_ref.shape[1]
    rounds = m // LANES
    work[...] = gram_ref[...]

    def refill(basis_t):
        image_t = dotf(basis_t, gram_ref[...], ((1,), (0,)))
        aug[:, pl.ds(0, r)] = dotf(image_t, image_t, ((1,), (1,)))
        aug[:, pl.ds(r, m)] = image_t

    refill(start_ref[...].T)
    for t in range(max(rounds, ITERS)):
        base = t * LANES

        def step(block, carry):
            if t < rounds:
                eliminate(work, base, base, m - base, block)
            if t < ITERS:
                eliminate(aug, 0, 0, r + m, block)
            return carry

        lax.fori_loop(0, LANES // SUB, step, 0)
        if t < rounds - 1:
            tail = m - base - LANES
            u = work[pl.ds(base, LANES), pl.ds(base + LANES, tail)]
            work[pl.ds(base + LANES, tail), pl.ds(base + LANES, tail)] -= dotf(u, u, ((0,), (0,)))
        if t < ITERS - 1:
            refill(aug[:, pl.ds(r, m)])
    basis_t = aug[:, pl.ds(r, m)]
    basis_ref[...] = basis_t
    factor_ref[...] = basis_t.T
    upper = work[...]
    row = lax.broadcasted_iota(jnp.int32, (m, m), 0)
    colm = lax.broadcasted_iota(jnp.int32, (m, m), 1)
    tri_ref[...] = jnp.where(row <= colm, upper, 0.0).T


def solve(gram, start_block):
    m, r = start_block.shape
    vmem = pl.BlockSpec(memory_space=pltpu.VMEM)
    return pl.pallas_call(
        solve_kernel,
        out_shape=(
            jax.ShapeDtypeStruct((m, m), F32),
            jax.ShapeDtypeStruct((m, r), F32),
            jax.ShapeDtypeStruct((r, m), F32),
        ),
        in_specs=[vmem, vmem],
        out_specs=(vmem, vmem, vmem),
        scratch_shapes=[pltpu.VMEM((m, m), F32), pltpu.VMEM((r, r + m), F32)],
        compiler_params=pltpu.CompilerParams(vmem_limit_bytes=32 * 1024 * 1024),
        name="solve",
    )(gram, start_block)


def per_device(unfolded, start_block):
    high = lax.Precision.HIGH
    rows_dev, cols_dev = unfolded.shape
    total_cols = cols_dev * lax.axis_size("rest")
    full_rows = lax.all_to_all(unfolded, "mode", split_axis=1, concat_axis=0, tiled=True)
    gram_part = jnp.dot(full_rows, full_rows.T, precision=high) / total_cols
    gram = lax.psum(gram_part, ("mode", "rest"))
    triangle, factor, basis_t = solve(gram, start_block)
    partial_value = jnp.dot(basis_t, full_rows, precision=high)
    core = lax.all_to_all(partial_value, "mode", split_axis=0, concat_axis=1, tiled=True)
    return (triangle, factor, core)


def solution(mesh):
    return jax.shard_map(
        per_device,
        mesh=mesh,
        in_specs=(P("mode", "rest"), P()),
        out_specs=(P(), P(), P("mode", "rest")),
        check_vma=False,
    )
```

profile of v0, /device:TPU:0, one launch (start us, length us, event | category | flops | bytes accessed | tf_op | source)
XLA Modules:
  0.0 295.3 jit_solution(3082099653523273584)
XLA Ops:
  7.2 0.0 all-reduce.2.cloned.1.call-start
  7.2 2.7 copy.11
  9.9 52.8 %all_to_all.35 = f32[128,4,2048]{2,0,1:T(8,128)S(1)} all-to-all(f32[128,4,2048]{2,0,1:T(8,128)S(1)} %bitcast.20), channel_id=1, replica_groups=mesh['mode'=4,'rest'=8] {'mode'}, dimensions={1} | all-to-all | bytes 8388608 | tf_op jit(solution)/shard_map/all_to_all | solution.py:127
  62.7 0.0 copy-start.2
  62.7 1.9 copy-done.2
  64.7 0.0 copy-start.1
  64.7 4.4 %convolution_multiply_fusion = f32[512,512]{1,0:T(8,128)} fusion(f32[512,2048]{1,0:T(8,128)S(1)} %bitcast.18), kind=kOutput, calls=%fused_computation.1 | convolution fusion | flops 3221487616 | bytes 5242880 | tf_op jit(solution)/shard_map/dot_general | solution.py:128
  69.1 0.0 all-reduce.2.cloned.1.call-update
  69.1 130.5 %all-reduce.2.cloned.1.call-done.gram_ref = f32[512,512]{1,0:T(8,128)} async-done(((f32[512,512]{1,0:T(8,128)}), f32[512,512]{1,0:T(8,128)}) %all-reduce.2.cloned.1.call-update) | async-done | bytes 1048592 | tf_op jit(solution)/shard_map/psum | solution.py:129
  199.6 0.0 copy-done.1
  199.6 0.0 copy-start
  199.6 1.2 copy-done
  200.9 66.9 %solve.1 = (f32[512,512]{1,0:T(8,128)}, f32[512,128]{1,0:T(8,128)}, f32[128,512]{1,0:T(8,128)S(1)}) custom-call(f32[512,512]{1,0:T(8,128)S(1)} %copy-done, f32[512,128]{1,0:T(8,128)S(1)} %copy-done.1), custom_call_target="tpu_custom_call" | custom-call | tf_op jit(solution)/shard_map/solve/pallas_call | solution.py:108
  267.8 3.6 %fusion = f32[4,32,2048]{2,1,0:T(8,128)S(1)} fusion(f32[4,32,512]{2,1,0:T(8,128)S(1)} %bitcast.17, f32[512,2048,1]{1,0,2:T(8,128)} %bitcast.19), kind=kOutput, calls=%fused_computation.2 | convolution fusion | flops 805306368 | bytes 5505024 | tf_op jit(solution)/shard_map/dot_general | solution.py:131
  271.4 16.0 %all_to_all.36 = f32[4,32,2048]{2,1,0:T(8,128)S(1)} all-to-all(f32[4,32,2048]{2,1,0:T(8,128)S(1)} %fusion), channel_id=1, replica_groups=mesh['mode'=4,'rest'=8] {'mode'}, dimensions={0} | all-to-all | bytes 2097152 | tf_op jit(solution)/shard_map/all_to_all | solution.py:132
  287.4 1.1 copy.9
Async XLA Ops:
  7.2 192.5 %all-reduce.2.cloned.1.call-start = ((), (), s32[]{:S(2)}) async-start(), calls=%async_computation.2 | async-start | bytes 2097152 | tf_op jit(solution)/shard_map/psum | solution.py:129
  62.7 1.9 copy-start.2
  64.7 135.0 %copy-start.1 = (f32[512,128]{1,0:T(8,128)S(1)}, f32[512,128]{1,0:T(8,128)}, u32[]{:S(2)}) copy-start(f32[512,128]{1,0:T(8,128)} %start_ref.1) | copy-start | bytes 786436
  199.6 1.2 copy-start
Sparse Core Ops, SparseCore 0:
  69.3 130.3 all-reduce.1
where the time goes:
time: 296 us; the launch traced here: 295 us
  waiting for transfers between devices  131 us (44%)
  blocking collectives  68.8 us (23%)
  Pallas kernels  66.9 us (23%)
  between operations  14 us (5%)
  matrix products  8.01 us (3%)
  local copies, waits for them, and re-layouts  6.9 us (2%)
    psum x1, waiting for transfers between devices, per_device(): gram = lax.psum(gram_part, ('mode', 'rest'))  130 us
    pallas_call x1, Pallas kernels, solve(): pl.pallas_call(solve_kernel, out_shape=(jax.ShapeDtypeStruct((m, m), F32)...  66.9 us
    all_to_all x1, blocking collectives, per_device(): lax.all_to_all(unfolded, 'mode', split_axis=1, concat_axis=0, tiled=True)  52.8 us
    all_to_all x1, blocking collectives, per_device(): lax.all_to_all(partial_value, 'mode', split_axis=0, concat_axis=1, tiled=...  16 us
  transfers between devices with their start and end apart: 1, of which 1 were waited for; matrix products, arithmetic and copies ran while one was open for 0% of the time, Pallas kernels for 0%

commit v1 on v0

--- a/solution.py
+++ b/solution.py
@@ -12,6 +12,7 @@
 LANES = 128
 F32 = jnp.float32
 BF16 = jnp.bfloat16
+MESH = pl.DeviceIdType.MESH
 
 
 def parts3(x):
@@ -64,11 +65,20 @@
     ref[pl.ds(row, LANES), pl.ds(col, width)] -= upd
 
 
-def solve_kernel(gram_ref, start_ref, tri_ref, factor_ref, basis_ref, work, aug):
-    m = gram_ref.shape[0]
-    r = start_ref.shape[1]
+def block_pairs(count):
+    return [(i, j) for i in range(count) for j in range(i, count)]
+
+
+def solve_kernel(packed_ref, start_ref, tri_ref, factor_ref, basis_ref, gram_ref, work, aug):
+    m, r = start_ref.shape
     rounds = m // LANES
-    work[...] = gram_ref[...]
+    for at, (i, j) in enumerate(block_pairs(rounds)):
+        piece = packed_ref[pl.ds(at * LANES, LANES), :]
+        spot = (pl.ds(i * LANES, LANES), pl.ds(j * LANES, LANES))
+        gram_ref[spot] = piece
+        work[spot] = piece
+        if i != j:
+            gram_ref[spot[::-1]] = piece.T
 
     def refill(basis_t):
         image_t = dotf(basis_t, gram_ref[...], ((1,), (0,)))
@@ -96,13 +106,19 @@
     basis_t = aug[:, pl.ds(r, m)]
     basis_ref[...] = basis_t
     factor_ref[...] = basis_t.T
-    upper = work[...]
-    row = lax.broadcasted_iota(jnp.int32, (m, m), 0)
-    colm = lax.broadcasted_iota(jnp.int32, (m, m), 1)
-    tri_ref[...] = jnp.where(row <= colm, upper, 0.0).T
-
-
-def solve(gram, start_block):
+    row = lax.broadcasted_iota(jnp.int32, (LANES, LANES), 0)
+    col = lax.broadcasted_iota(jnp.int32, (LANES, LANES), 1)
+    for i in range(rounds):
+        for j in range(rounds):
+            spot = (pl.ds(j * LANES, LANES), pl.ds(i * LANES, LANES))
+            if j < i:
+                tri_ref[spot] = jnp.zeros((LANES, LANES), F32)
+                continue
+            piece = work[spot[::-1]]
+            tri_ref[spot] = (jnp.where(row <= col, piece, 0.0) if i == j else piece).T
+
+
+def solve(packed, start_block):
     m, r = start_block.shape
     vmem = pl.BlockSpec(memory_space=pltpu.VMEM)
     return pl.pallas_call(
@@ -114,10 +130,108 @@
         ),
         in_specs=[vmem, vmem],
         out_specs=(vmem, vmem, vmem),
-        scratch_shapes=[pltpu.VMEM((m, m), F32), pltpu.VMEM((r, r + m), F32)],
+        scratch_shapes=[pltpu.VMEM((m, m), F32), pltpu.VMEM((m, m), F32), pltpu.VMEM((r, r + m), F32)],
         compiler_params=pltpu.CompilerParams(vmem_limit_bytes=32 * 1024 * 1024),
         name="solve",
-    )(gram, start_block)
+    )(packed, start_block)
+
+
+def sum_kernel(shape, in_ref, out_ref, got1, got2, got3, sum1, sum2, send, recv):
+    modes, cores, depth = shape
+    me_mode = lax.axis_index("mode")
+    me_rest = lax.axis_index("rest")
+    me_core = lax.rem(me_rest, cores)
+    me_z = me_rest // cores
+    mine = (me_core, me_mode, me_z)
+    sizes = (cores, modes, depth)
+    rows = [in_ref.shape[0] // cores]
+    rows.append(rows[0] // modes)
+    rows.append(rows[1] // depth)
+
+    def peer(stage, off):
+        other = lax.rem(mine[stage] + off, sizes[stage])
+        spot = [me_core, me_mode, me_z]
+        spot[stage] = other
+        return other, (spot[1], spot[2] * cores + spot[0])
+
+    barrier = pltpu.get_barrier_semaphore()
+    for stage in range(3):
+        def greet(off, carry):
+            _, device = peer(stage, off)
+            pl.semaphore_signal(barrier, inc=1, device_id=device, device_id_type=MESH)
+            return carry
+        lax.fori_loop(1, sizes[stage], greet, 0)
+    pl.semaphore_wait(barrier, sum(sizes) - 3)
+
+    def at(start, size):
+        return pl.ds(pl.multiple_of(start, SUB), size)
+
+    def exchange(phase, stage, source, target):
+        def copy(off):
+            other, device = peer(stage, off)
+            return pltpu.make_async_remote_copy(
+                src_ref=source(other),
+                dst_ref=target(mine[stage], off),
+                send_sem=send.at[phase, off],
+                recv_sem=recv.at[phase, off],
+                device_id=device,
+                device_id_type=MESH,
+            )
+        def begin(off, carry):
+            copy(off).start()
+            return carry
+        def end(off, carry):
+            copy(off).wait()
+            return carry
+        lax.fori_loop(1, sizes[stage], begin, 0)
+        lax.fori_loop(1, sizes[stage], end, 0)
+
+    def total(stage, source, got):
+        def add(off, value):
+            return value + got[off - 1]
+        return lax.fori_loop(1, sizes[stage], add, source[at(mine[stage] * rows[stage], rows[stage]), :])
+
+    exchange(0, 0, lambda o: in_ref.at[at(o * rows[0], rows[0])], lambda o, off: got1.at[off - 1])
+    sum1[...] = total(0, in_ref, got1)
+    exchange(1, 1, lambda o: sum1.at[at(o * rows[1], rows[1])], lambda o, off: got2.at[off - 1])
+    sum2[...] = total(1, sum1, got2)
+    exchange(2, 2, lambda o: sum2.at[at(o * rows[2], rows[2])], lambda o, off: got3.at[off - 1])
+    start2 = me_core * rows[0] + me_mode * rows[1]
+    start3 = start2 + me_z * rows[2]
+    out_ref[at(start3, rows[2]), :] = total(2, sum2, got3)
+    for phase, stage, start, size in ((3, 2, start3, rows[2]), (4, 1, start2, rows[1]), (5, 0, me_core * rows[0], rows[0])):
+        block = out_ref.at[at(start, size)]
+        exchange(phase, stage, lambda o: block, lambda o, off: block)
+
+
+def sum_all(packed, modes, rest):
+    cores = 2 if rest % 2 == 0 else 1
+    depth = rest // cores
+    count = packed.shape[0]
+    each = pl.cdiv(count, modes * rest * SUB) * SUB
+    padded = each * modes * rest
+    if padded != count:
+        packed = jnp.pad(packed, ((0, padded - count), (0, 0)))
+    width = packed.shape[1]
+    vmem = pl.BlockSpec(memory_space=pltpu.VMEM)
+    most = max(cores, modes, depth)
+    return pl.pallas_call(
+        functools.partial(sum_kernel, (modes, cores, depth)),
+        out_shape=jax.ShapeDtypeStruct((padded, width), F32),
+        in_specs=[vmem],
+        out_specs=vmem,
+        scratch_shapes=[
+            pltpu.VMEM((max(cores - 1, 1), padded // cores, width), F32),
+            pltpu.VMEM((max(modes - 1, 1), padded // (cores * modes), width), F32),
+            pltpu.VMEM((max(depth - 1, 1), each, width), F32),
+            pltpu.VMEM((padded // cores, width), F32),
+            pltpu.VMEM((padded // (cores * modes), width), F32),
+            pltpu.SemaphoreType.DMA((6, most)),
+            pltpu.SemaphoreType.DMA((6, most)),
+        ],
+        compiler_params=pltpu.CompilerParams(collective_id=0, has_side_effects=True),
+        name="sum_all",
+    )(packed)[:count]
 
 
 def per_device(unfolded, start_block):
@@ -125,9 +239,14 @@
     rows_dev, cols_dev = unfolded.shape
     total_cols = cols_dev * lax.axis_size("rest")
     full_rows = lax.all_to_all(unfolded, "mode", split_axis=1, concat_axis=0, tiled=True)
-    gram_part = jnp.dot(full_rows, full_rows.T, precision=high) / total_cols
-    gram = lax.psum(gram_part, ("mode", "rest"))
-    triangle, factor, basis_t = solve(gram, start_block)
+    blocks = full_rows.shape[0] // LANES
+    pieces = []
+    for i in range(blocks):
+        strip = jnp.dot(full_rows[i * LANES : (i + 1) * LANES], full_rows[i * LANES :].T, precision=high) / total_cols
+        pieces += [strip[:, j * LANES : (j + 1) * LANES] for j in range(blocks - i)]
+    packed = jnp.concatenate(pieces, axis=0)
+    packed = sum_all(packed, lax.axis_size("mode"), lax.axis_size("rest"))
+    triangle, factor, basis_t = solve(packed, start_block)
     partial_value = jnp.dot(basis_t, full_rows, precision=high)
     core = lax.all_to_all(partial_value, "mode", split_axis=0, concat_axis=1, tiled=True)
     return (triangle, factor, core)

time: 296 us -> 181 us (0.61)
  waiting for transfers between devices: 131 us -> 0 us
  Pallas kernels: 66.9 us -> 93.7 us
  between operations: 14 us -> 0.81 us
    psum x1 -> x0, waiting for transfers between devices: 130 us -> none  [per_device(): gram = lax.psum(gram_part, ('mode', 'rest'))]
    pallas_call x0 -> x1, Pallas kernels: none -> 26.7 us  [sum_all(): pl.pallas_call(functools.partial(sum_kernel, (modes, cores, depth)), out_...]
  transfers between devices with their start and end apart: 1 -> 0, of which waited for: 1 -> 0; matrix products, arithmetic and copies ran while one was open for 0% -> 0% of each run, Pallas kernels for 0% -> 0%
where the time goes in v1:
time: 181 us; the launch traced here: 180 us
  Pallas kernels  93.7 us (52%)
  blocking collectives  70.2 us (39%)
  matrix products  9.35 us (5%)
  local copies, waits for them, and re-layouts  6.09 us (3%)
    pallas_call x1, Pallas kernels, solve(): pl.pallas_call(solve_kernel, out_shape=(jax.ShapeDtypeStruct((m, m), F32)...  67 us
    all_to_all x1, blocking collectives, per_device(): lax.all_to_all(unfolded, 'mode', split_axis=1, concat_axis=0, tiled=True)  52.8 us
    pallas_call x1, Pallas kernels, sum_all(): pl.pallas_call(functools.partial(sum_kernel, (modes, cores, depth)), out_...  26.7 us
    all_to_all x1, blocking collectives, per_device(): lax.all_to_all(partial_value, 'mode', split_axis=0, concat_axis=1, tiled=...  17.4 us
    dot_general x4, matrix products, per_device(): jnp.dot(full_rows[i * LANES:(i + 1) * LANES], full_rows[i * LANES:].T, pr...  5.79 us

profile of v1, /device:TPU:0, one launch (start us, length us, event | category | flops | bytes accessed | tf_op | source)
XLA Modules:
  0.0 180.2 jit_solution(925684483033496775)
XLA Ops:
  0.6 2.5 %copy.11 = f32[16,4,8,2048]{3,2,0,1:T(8,128)S(1)} copy(f32[16,4,8,2048]{3,2,1,0:T(8,128)} %bitcast.44) | data formatting | bytes 8388608 | tf_op jit(solution)/shard_map/all_to_all | solution.py:241
  3.1 52.8 %all_to_all.35 = f32[128,4,2048]{2,0,1:T(8,128)S(1)} all-to-all(f32[128,4,2048]{2,0,1:T(8,128)S(1)} %bitcast.41), channel_id=1, replica_groups=mesh['mode'=4,'rest'=8] {'mode'}, dimensions={1} | all-to-all | bytes 8388608 | tf_op jit(solution)/shard_map/all_to_all | solution.py:241
  55.9 0.0 copy-start.2
  55.9 0.2 slice.96
  56.2 0.3 slice.91
  56.5 2.3 %convolution_multiply_fusion = f32[128,512]{1,0:T(8,128)S(1)} fusion(f32[512,2048]{1,0:T(8,128)S(1)} %bitcast.35, f32[4,128,2048]{2,1,0:T(8,128)S(1)} %bitcast.36), kind=kOutput, calls=%fused_computation.1 | convolution fusion | flops 805371904 | bytes 5505024 | tf_op jit(solution)/shard_map/dot_general | solution.py:245
  58.9 1.2 convolution_multiply_fusion.2
  60.1 0.0 copy-start.1
  60.1 1.6 convolution_multiply_fusion.1
  61.9 0.0 copy-done.2
  61.9 0.6 fusion.in_ref
  62.5 0.0 copy-start.3
  62.5 0.8 copy-done.3
  63.3 26.7 %sum_all.1.packed_ref = f32[1280,128]{1,0:T(8,128)} custom-call(f32[1280,128]{1,0:T(8,128)} %copy-done.3), custom_call_target="tpu_custom_call" | custom-call | tf_op jit(solution)/shard_map/sum_all/pallas_call | solution.py:218
  90.1 0.0 copy-done.1
  90.1 0.0 copy-start
  90.1 1.1 copy-done
  91.2 67.0 %solve.1 = (f32[512,512]{1,0:T(8,128)}, f32[512,128]{1,0:T(8,128)}, f32[128,512]{1,0:T(8,128)S(1)}) custom-call(f32[1280,128]{1,0:T(8,128)S(1)} %copy-done, f32[512,128]{1,0:T(8,128)S(1)} %copy-done.1), custom_call_target="tpu_custom_call" | custom-call | tf_op jit(solution)/shard_map/solve/pallas_call | solution.py:124
  158.2 3.6 %fusion.1 = f32[4,32,2048]{2,1,0:T(8,128)S(1)} fusion(f32[4,32,512]{2,1,0:T(8,128)S(1)} %bitcast.32, f32[512,2048,1]{1,0,2:T(8,128)} %bitcast.40), kind=kOutput, calls=%fused_computation.19 | convolution fusion | flops 805306368 | bytes 5505024 | tf_op jit(solution)/shard_map/dot_general | solution.py:250
  161.7 17.4 %all_to_all.36 = f32[4,32,2048]{2,1,0:T(8,128)S(1)} all-to-all(f32[4,32,2048]{2,1,0:T(8,128)S(1)} %fusion.1), channel_id=1, replica_groups=mesh['mode'=4,'rest'=8] {'mode'}, dimensions={0} | all-to-all | bytes 2097152 | tf_op jit(solution)/shard_map/all_to_all | solution.py:251
  179.1 1.1 copy.9
  (9 shorter events, 0.1 us)
Async XLA Ops:
  55.9 5.9 %copy-start.2 = (f32[128,4,2048]{2,0,1:T(8,128)}, f32[128,4,2048]{2,0,1:T(8,128)S(1)}, u32[]{:S(2)}) copy-start(f32[128,4,2048]{2,0,1:T(8,128)S(1)} %all_to_all.35) | copy-start | bytes 12582916
  60.1 30.0 %copy-start.1 = (f32[512,128]{1,0:T(8,128)S(1)}, f32[512,128]{1,0:T(8,128)}, u32[]{:S(2)}) copy-start(f32[512,128]{1,0:T(8,128)} %start_ref.1) | copy-start | bytes 786436
  62.5 0.8 copy-start.3
  90.1 1.1 copy-start

commit v2 on v1

--- a/solution.py
+++ b/solution.py
@@ -9,6 +9,7 @@
 
 ITERS = 3
 SUB = 8
+STEP = 16
 LANES = 128
 F32 = jnp.float32
 BF16 = jnp.bfloat16
@@ -38,25 +39,27 @@
 
 
 def eliminate(ref, row, col, width, block):
-    r0 = pl.multiple_of(block * SUB, SUB)
-    v = ref[pl.ds(row + r0, SUB), pl.ds(col, width)]
-    sub = lax.broadcasted_iota(jnp.int32, (SUB, 1), 0)
-    d = pltpu.roll(v[:, :LANES], lax.rem(LANES - r0, LANES), 1)
-    pivots = jnp.ones((SUB, 1), F32)
-    for k in range(SUB):
-        c = d[:, k : k + 1]
-        p = c[k : k + 1, :]
-        f = jnp.where(sub > k, c / p, 0.0)
+    r0 = pl.multiple_of(block * STEP, STEP)
+    chunks = [ref[pl.ds(row + r0, STEP), pl.ds(col + c, LANES)] for c in range(0, width, LANES)]
+    sub = lax.broadcasted_iota(jnp.int32, (STEP, LANES), 0)
+    cols = [
+        jnp.take_along_axis(chunks[0], jnp.full((STEP, LANES), r0 + k, jnp.int32), axis=1) for k in range(STEP)
+    ]
+    pivots = jnp.ones((STEP, LANES), F32)
+    for k in range(STEP):
+        p = cols[k][k : k + 1, :]
+        f = jnp.where(sub > k, cols[k] * (1.0 / p), 0.0)
         pivots = jnp.where(sub == k, p, pivots)
-        if k < SUB - 1:
-            d = d - f * d[k : k + 1, :]
-            v = v - f * v[k : k + 1, :]
+        for j in range(k + 1, STEP):
+            cols[j] = cols[j] - f * cols[j][k : k + 1, :]
+        chunks = [v - f * v[k : k + 1, :] for v in chunks]
     s = lax.rsqrt(pivots)
     s = s * (1.5 - 0.5 * pivots * s * s)
-    v = v * s
-    ref[pl.ds(row + r0, SUB), pl.ds(col, width)] = v
-    lane = lax.broadcasted_iota(jnp.int32, (SUB, LANES), 1)
-    keep = lane >= r0 + SUB
+    chunks = [v * s for v in chunks]
+    v = jnp.concatenate(chunks, axis=1)
+    ref[pl.ds(row + r0, STEP), pl.ds(col, width)] = v
+    lane = lax.broadcasted_iota(jnp.int32, (STEP, LANES), 1)
+    keep = lane >= r0 + STEP
     hi, mid, lo = parts3(v)
     lh, lm, ll = (jnp.where(keep, x[:, :LANES], 0.0) for x in (hi, mid, lo))
     left = jnp.concatenate([lh, lh, lm, lm, lh, ll], axis=0).astype(BF16)
@@ -96,7 +99,7 @@
                 eliminate(aug, 0, 0, r + m, block)
             return carry
 
-        lax.fori_loop(0, LANES // SUB, step, 0)
+        lax.fori_loop(0, LANES // STEP, step, 0)
         if t < rounds - 1:
             tail = m - base - LANES
             u = work[pl.ds(base, LANES), pl.ds(base + LANES, tail)]

time: 181 us -> 137 us (0.76)
  Pallas kernels: 93.7 us -> 50.7 us
    pallas_call x1, Pallas kernels: 67 us -> 23.9 us  [solve(): pl.pallas_call(solve_kernel, out_shape=(jax.ShapeDtypeStruct((m, m), F32)...]
where the time goes in v2:
time: 137 us
  blocking collectives  70.2 us (51%)
  Pallas kernels  50.7 us (37%)
  matrix products  9.35 us (7%)
  local copies, waits for them, and re-layouts  6.09 us (4%)
    all_to_all x1, blocking collectives, per_device(): lax.all_to_all(unfolded, 'mode', split_axis=1, concat_axis=0, tiled=True)  52.8 us
    pallas_call x1, Pallas kernels, sum_all(): pl.pallas_call(functools.partial(sum_kernel, (modes, cores, depth)), out_...  26.7 us
    pallas_call x1, Pallas kernels, solve(): pl.pallas_call(solve_kernel, out_shape=(jax.ShapeDtypeStruct((m, m), F32)...  23.9 us
    all_to_all x1, blocking collectives, per_device(): lax.all_to_all(partial_value, 'mode', split_axis=0, concat_axis=1, tiled=...  17.4 us
    dot_general x4, matrix products, per_device(): jnp.dot(full_rows[i * LANES:(i + 1) * LANES], full_rows[i * LANES:].T, pr...  5.79 us
    dot_general x1, matrix products, per_device(): partial_value = jnp.dot(basis_t, full_rows, precision=high)  3.57 us

profile of v2, /device:TPU:0, one launch (start us, length us, event | category | flops | bytes accessed | tf_op | source)
XLA Modules:
  0.0 137.1 jit_solution(394781727528196682)
XLA Ops:
  0.6 2.5 %copy.11 = f32[16,4,8,2048]{3,2,0,1:T(8,128)S(1)} copy(f32[16,4,8,2048]{3,2,1,0:T(8,128)} %bitcast.44) | data formatting | bytes 8388608 | tf_op jit(solution)/shard_map/all_to_all | solution.py:244
  3.1 52.8 %all_to_all.35 = f32[128,4,2048]{2,0,1:T(8,128)S(1)} all-to-all(f32[128,4,2048]{2,0,1:T(8,128)S(1)} %bitcast.41), channel_id=1, replica_groups=mesh['mode'=4,'rest'=8] {'mode'}, dimensions={1} | all-to-all | bytes 8388608 | tf_op jit(solution)/shard_map/all_to_all | solution.py:244
  55.9 0.0 copy-start.2
  55.9 0.2 slice.96
  56.2 0.3 slice.91
  56.5 2.3 %convolution_multiply_fusion = f32[128,512]{1,0:T(8,128)S(1)} fusion(f32[512,2048]{1,0:T(8,128)S(1)} %bitcast.35, f32[4,128,2048]{2,1,0:T(8,128)S(1)} %bitcast.36), kind=kOutput, calls=%fused_computation.1 | convolution fusion | flops 805371904 | bytes 5505024 | tf_op jit(solution)/shard_map/dot_general | solution.py:248
  58.9 1.2 convolution_multiply_fusion.2
  60.1 0.0 copy-start.1
  60.1 1.6 %convolution_multiply_fusion.1 = f32[128,384]{1,0:T(8,128)S(1)} fusion(f32[384,2048]{1,0:T(8,128)S(1)} %bitcast.42, f32[4,128,2048]{2,1,0:T(8,128)S(1)} %bitcast.38), kind=kOutput, calls=%fused_computation.2 | convolution fusion | flops 604028928 | bytes 4390912 | tf_op jit(solution)/shard_map/dot_general | solution.py:248
  61.9 0.0 copy-done.2
  61.9 0.6 fusion.in_ref
  62.5 0.0 copy-start.3
  62.5 0.8 copy-done.3
  63.3 26.7 %sum_all.1.packed_ref = f32[1280,128]{1,0:T(8,128)} custom-call(f32[1280,128]{1,0:T(8,128)} %copy-done.3), custom_call_target="tpu_custom_call" | custom-call | tf_op jit(solution)/shard_map/sum_all/pallas_call | solution.py:221
  90.1 0.0 copy-done.1
  90.1 0.0 copy-start
  90.1 1.1 copy-done
  91.2 23.9 %solve.1 = (f32[512,512]{1,0:T(8,128)}, f32[512,128]{1,0:T(8,128)}, f32[128,512]{1,0:T(8,128)S(1)}) custom-call(f32[1280,128]{1,0:T(8,128)S(1)} %copy-done, f32[512,128]{1,0:T(8,128)S(1)} %copy-done.1), custom_call_target="tpu_custom_call" | custom-call | tf_op jit(solution)/shard_map/solve/pallas_call | solution.py:127
  115.1 3.6 %fusion.1 = f32[4,32,2048]{2,1,0:T(8,128)S(1)} fusion(f32[4,32,512]{2,1,0:T(8,128)S(1)} %bitcast.32, f32[512,2048,1]{1,0,2:T(8,128)} %bitcast.40), kind=kOutput, calls=%fused_computation.19 | convolution fusion | flops 805306368 | bytes 5505024 | tf_op jit(solution)/shard_map/dot_general | solution.py:253
  118.7 17.4 %all_to_all.36 = f32[4,32,2048]{2,1,0:T(8,128)S(1)} all-to-all(f32[4,32,2048]{2,1,0:T(8,128)S(1)} %fusion.1), channel_id=1, replica_groups=mesh['mode'=4,'rest'=8] {'mode'}, dimensions={0} | all-to-all | bytes 2097152 | tf_op jit(solution)/shard_map/all_to_all | solution.py:254
  136.1 1.1 copy.9
  (9 shorter events, 0.1 us)
Async XLA Ops:
  55.9 5.9 %copy-start.2 = (f32[128,4,2048]{2,0,1:T(8,128)}, f32[128,4,2048]{2,0,1:T(8,128)S(1)}, u32[]{:S(2)}) copy-start(f32[128,4,2048]{2,0,1:T(8,128)S(1)} %all_to_all.35) | copy-start | bytes 12582916
  60.1 30.0 %copy-start.1 = (f32[512,128]{1,0:T(8,128)S(1)}, f32[512,128]{1,0:T(8,128)}, u32[]{:S(2)}) copy-start(f32[512,128]{1,0:T(8,128)} %start_ref.1) | copy-start | bytes 786436
  62.5 0.8 copy-start.3
  90.1 1.1 copy-start

commit v3 on v2

--- a/solution.py
+++ b/solution.py
@@ -10,6 +10,7 @@
 ITERS = 3
 SUB = 8
 STEP = 16
+CHUNKS = 4
 LANES = 128
 F32 = jnp.float32
 BF16 = jnp.bfloat16
@@ -23,13 +24,8 @@
     return hi, mid, rest - mid
 
 
-def dot3(x, y, dims):
-    xh = x.astype(BF16)
-    xl = (x - xh.astype(F32)).astype(BF16)
-    yh = y.astype(BF16)
-    yl = (y - yh.astype(F32)).astype(BF16)
-    dot = functools.partial(lax.dot_general, dimension_numbers=(dims, ((), ())), preferred_element_type=F32)
-    return dot(xh, yh) + (dot(xh, yl) + dot(xl, yh))
+def nt(x, y):
+    return lax.dot_general(x, y, (((1,), (1,)), ((), ())), preferred_element_type=F32)
 
 
 def dotf(x, y, dims):
@@ -139,7 +135,8 @@
     )(packed, start_block)
 
 
-def sum_kernel(shape, in_ref, out_ref, got1, got2, got3, sum1, sum2, send, recv):
+def gram_kernel(shape, total_cols, x_ref, full_out, out_ref, full, in_ref, got1, got2, got3, sum1, sum2,
+                send, recv, row_send, row_recv, row_local, row_out):
     modes, cores, depth = shape
     me_mode = lax.axis_index("mode")
     me_rest = lax.axis_index("rest")
@@ -165,6 +162,50 @@
             return carry
         lax.fori_loop(1, sizes[stage], greet, 0)
     pl.semaphore_wait(barrier, sum(sizes) - 3)
+
+    rows_dev = x_ref.shape[0]
+    m, width = full.shape
+    chunk = width // CHUNKS
+    copies = []
+    for c in range(CHUNKS):
+        batch = []
+        spot = (pl.ds(pl.multiple_of(me_mode * rows_dev, rows_dev), rows_dev), pl.ds(c * chunk, chunk))
+        for off in range(1, modes):
+            other, device = peer(1, off)
+            batch.append(pltpu.make_async_remote_copy(
+                src_ref=x_ref.at[:, pl.ds(pl.multiple_of(other * width + c * chunk, chunk), chunk)],
+                dst_ref=full.at[spot],
+                send_sem=row_send.at[c, off],
+                recv_sem=row_recv.at[c, off],
+                device_id=device,
+                device_id_type=MESH,
+            ))
+        batch.append(pltpu.make_async_copy(
+            x_ref.at[:, pl.ds(pl.multiple_of(me_mode * width + c * chunk, chunk), chunk)], full.at[spot], row_local.at[c]
+        ))
+        for copy in batch:
+            copy.start()
+        copies.append(batch)
+    pairs = block_pairs(m // LANES)
+    in_ref[...] = jnp.zeros_like(in_ref)
+    stores = []
+    for c in range(CHUNKS):
+        for copy in copies[c]:
+            copy.wait()
+        part = (slice(None), pl.ds(c * chunk, chunk))
+        store = pltpu.make_async_copy(full.at[part], full_out.at[part], row_out.at[c])
+        store.start()
+        stores.append(store)
+        x = full[part]
+        hi = x.astype(BF16)
+        lo = (x - hi.astype(F32)).astype(BF16)
+        for i in range(m // LANES):
+            top = slice(i * LANES, (i + 1) * LANES)
+            strip = nt(hi[top], hi[i * LANES :]) + (nt(hi[top], lo[i * LANES :]) + nt(lo[top], hi[i * LANES :]))
+            for j in range(i, m // LANES):
+                spot = pl.ds(pairs.index((i, j)) * LANES, LANES)
+                in_ref[spot, :] += strip[:, (j - i) * LANES : (j - i + 1) * LANES]
+    in_ref[...] = in_ref[...] / total_cols
 
     def at(start, size):
         return pl.ds(pl.multiple_of(start, SUB), size)
@@ -207,48 +248,52 @@
         exchange(phase, stage, lambda o: block, lambda o, off: block)
 
 
-def sum_all(packed, modes, rest):
+    for store in stores:
+        store.wait()
+
+
+def gram_sum(unfolded, modes, rest):
+    rows_dev, cols_dev = unfolded.shape
+    m, width = rows_dev * modes, cols_dev // modes
     cores = 2 if rest % 2 == 0 else 1
     depth = rest // cores
-    count = packed.shape[0]
+    count = len(block_pairs(m // LANES)) * LANES
     each = pl.cdiv(count, modes * rest * SUB) * SUB
     padded = each * modes * rest
-    if padded != count:
-        packed = jnp.pad(packed, ((0, padded - count), (0, 0)))
-    width = packed.shape[1]
     vmem = pl.BlockSpec(memory_space=pltpu.VMEM)
+    anywhere = pl.BlockSpec(memory_space=pl.ANY)
     most = max(cores, modes, depth)
     return pl.pallas_call(
-        functools.partial(sum_kernel, (modes, cores, depth)),
-        out_shape=jax.ShapeDtypeStruct((padded, width), F32),
-        in_specs=[vmem],
-        out_specs=vmem,
+        functools.partial(gram_kernel, (modes, cores, depth), cols_dev * rest),
+        out_shape=(jax.ShapeDtypeStruct((m, width), F32), jax.ShapeDtypeStruct((padded, LANES), F32)),
+        in_specs=[anywhere],
+        out_specs=(anywhere, vmem),
         scratch_shapes=[
-            pltpu.VMEM((max(cores - 1, 1), padded // cores, width), F32),
-            pltpu.VMEM((max(modes - 1, 1), padded // (cores * modes), width), F32),
-            pltpu.VMEM((max(depth - 1, 1), each, width), F32),
-            pltpu.VMEM((padded // cores, width), F32),
-            pltpu.VMEM((padded // (cores * modes), width), F32),
+            pltpu.VMEM((m, width), F32),
+            pltpu.VMEM((padded, LANES), F32),
+            pltpu.VMEM((max(cores - 1, 1), padded // cores, LANES), F32),
+            pltpu.VMEM((max(modes - 1, 1), padded // (cores * modes), LANES), F32),
+            pltpu.VMEM((max(depth - 1, 1), each, LANES), F32),
+            pltpu.VMEM((padded // cores, LANES), F32),
+            pltpu.VMEM((padded // (cores * modes), LANES), F32),
             pltpu.SemaphoreType.DMA((6, most)),
             pltpu.SemaphoreType.DMA((6, most)),
+            pltpu.SemaphoreType.DMA((CHUNKS, modes)),
+            pltpu.SemaphoreType.DMA((CHUNKS, modes)),
+            pltpu.SemaphoreType.DMA((CHUNKS,)),
+            pltpu.SemaphoreType.DMA((CHUNKS,)),
         ],
-        compiler_params=pltpu.CompilerParams(collective_id=0, has_side_effects=True),
-        name="sum_all",
-    )(packed)[:count]
+        compiler_params=pltpu.CompilerParams(
+            collective_id=0, has_side_effects=True, vmem_limit_bytes=32 * 1024 * 1024
+        ),
+        name="gram_sum",
+    )(unfolded)
 
 
 def per_device(unfolded, start_block):
     high = lax.Precision.HIGH
-    rows_dev, cols_dev = unfolded.shape
-    total_cols = cols_dev * lax.axis_size("rest")
-    full_rows = lax.all_to_all(unfolded, "mode", split_axis=1, concat_axis=0, tiled=True)
-    blocks = full_rows.shape[0] // LANES
-    pieces = []
-    for i in range(blocks):
-        strip = jnp.dot(full_rows[i * LANES : (i + 1) * LANES], full_rows[i * LANES :].T, precision=high) / total_cols
-        pieces += [strip[:, j * LANES : (j + 1) * LANES] for j in range(blocks - i)]
-    packed = jnp.concatenate(pieces, axis=0)
-    packed = sum_all(packed, lax.axis_size("mode"), lax.axis_size("rest"))
+    modes, rest = lax.axis_size("mode"), lax.axis_size("rest")
+    full_rows, packed = gram_sum(unfolded, modes, rest)
     triangle, factor, basis_t = solve(packed, start_block)
     partial_value = jnp.dot(basis_t, full_rows, precision=high)
     core = lax.all_to_all(partial_value, "mode", split_axis=0, concat_axis=1, tiled=True)

time: 137 us -> 123 us (0.90)
  blocking collectives: 70.2 us -> 17.4 us
  Pallas kernels: 50.7 us -> 99.8 us
  matrix products: 9.35 us -> 1.49 us
  local copies, waits for them, and re-layouts: 6.09 us -> 3.25 us
    all_to_all x1 -> x0, blocking collectives: 52.8 us -> none  [per_device(): lax.all_to_all(unfolded, 'mode', split_axis=1, concat_axis=0, tiled=True)]
    pallas_call x1, Pallas kernels: 26.7 us -> 75.9 us  [gram_sum(): pl.pallas_call(functools.partial(gram_kernel, (modes, cores, depth), cols...]
    dot_general x4 -> x0, matrix products: 5.79 us -> none  [per_device(): jnp.dot(full_rows[i * LANES:(i + 1) * LANES], full_rows[i * LANES:].T, pr...]
    all_to_all x1 -> x0, local copies, waits for them, and re-layouts: 2.46 us -> none  [per_device(): lax.all_to_all(unfolded, 'mode', split_axis=1, concat_axis=0, tiled=True)]
    dot_general x1, matrix products: 3.57 us -> 1.49 us  [per_device(): partial_value = jnp.dot(basis_t, full_rows, precision=high)]
where the time goes in v3:
time: 123 us
  Pallas kernels  99.8 us (81%)
  blocking collectives  17.4 us (14%)
  local copies, waits for them, and re-layouts  3.25 us (3%)
  matrix products  1.49 us (1%)
    pallas_call x1, Pallas kernels, gram_sum(): pl.pallas_call(functools.partial(gram_kernel, (modes, cores, depth), cols...  75.9 us
    pallas_call x1, Pallas kernels, solve(): pl.pallas_call(solve_kernel, out_shape=(jax.ShapeDtypeStruct((m, m), F32)...  23.9 us
    all_to_all x1, blocking collectives, per_device(): lax.all_to_all(partial_value, 'mode', split_axis=0, concat_axis=1, tiled=...  17.4 us

profile of v3, /device:TPU:0, one launch (start us, length us, event | category | flops | bytes accessed | tf_op | source)
XLA Modules:
  0.0 122.6 jit_solution(15019881536328916440)
XLA Ops:
  0.6 0.0 copy-start
  0.6 2.2 %copy-done = f32[128,8192]{1,0:T(8,128)S(1)} copy-done((f32[128,8192]{1,0:T(8,128)S(1)}, f32[128,8192]{1,0:T(8,128)}, u32[]{:S(2)}) %copy-start) | copy-done | bytes 4194328
  2.8 0.0 copy-start.1
  2.8 75.9 %gram_sum.1 = (f32[512,2048]{1,0:T(8,128)S(1)}, f32[1280,128]{1,0:T(8,128)S(1)}) custom-call(f32[128,8192]{1,0:T(8,128)S(1)} %copy-done), custom_call_target="tpu_custom_call" | custom-call | tf_op jit(solution)/shard_map/gram_sum/pallas_call | solution.py:266
  78.7 0.0 copy-done.1
  78.7 23.9 %solve.1 = (f32[512,512]{1,0:T(8,128)}, f32[512,128]{1,0:T(8,128)}, f32[128,512]{1,0:T(8,128)S(1)}) custom-call(f32[1280,128]{1,0:T(8,128)S(1)} %get-tuple-element.8.packed_ref, f32[512,128]{1,0:T(8,128)S(1)} %copy-done.1), custom_call_target="tpu_custom_call" | custom-call | tf_op jit(solution)/shard_map/solve/pallas_call | solution.py:123
  102.6 1.5 %fusion = f32[128,2048]{1,0:T(8,128)S(1)} fusion(f32[128,512]{1,0:T(8,128)S(1)} %get-tuple-element.11, f32[512,2048]{1,0:T(8,128)S(1)} %get-tuple-element.12), kind=kOutput, calls=%fused_computation | convolution fusion | flops 805306368 | bytes 5505024 | tf_op jit(solution)/shard_map/dot_general | solution.py:298
  104.2 17.4 %all_to_all.19 = f32[4,32,2048]{2,1,0:T(8,128)S(1)} all-to-all(f32[4,32,2048]{2,1,0:T(8,128)S(1)} %bitcast.7), channel_id=1, replica_groups=mesh['mode'=4,'rest'=8] {'mode'}, dimensions={0} | all-to-all | bytes 2097152 | tf_op jit(solution)/shard_map/all_to_all | solution.py:299
  121.5 1.1 copy.6
Async XLA Ops:
  0.6 2.2 %copy-start = (f32[128,8192]{1,0:T(8,128)S(1)}, f32[128,8192]{1,0:T(8,128)}, u32[]{:S(2)}) copy-start(f32[128,8192]{1,0:T(8,128)} %x_ref.1) | copy-start | bytes 12582916
  2.8 75.9 %copy-start.1 = (f32[512,128]{1,0:T(8,128)S(1)}, f32[512,128]{1,0:T(8,128)}, u32[]{:S(2)}) copy-start(f32[512,128]{1,0:T(8,128)} %start_ref.1) | copy-start | bytes 786436

commit v4 on v3

--- a/solution.py
+++ b/solution.py
@@ -26,6 +26,10 @@
 
 def nt(x, y):
     return lax.dot_general(x, y, (((1,), (1,)), ((), ())), preferred_element_type=F32)
+
+
+def nn(x, y):
+    return lax.dot_general(x, y, (((1,), (0,)), ((), ())), preferred_element_type=F32)
 
 
 def dotf(x, y, dims):
@@ -68,7 +72,7 @@
     return [(i, j) for i in range(count) for j in range(i, count)]
 
 
-def solve_kernel(packed_ref, start_ref, tri_ref, factor_ref, basis_ref, gram_ref, work, aug):
+def solve_kernel(packed_ref, start_ref, work, factor_ref, basis_ref, gram_ref, aug):
     m, r = start_ref.shape
     rounds = m // LANES
     for at, (i, j) in enumerate(block_pairs(rounds)):
@@ -85,11 +89,11 @@
         aug[:, pl.ds(r, m)] = image_t
 
     refill(start_ref[...].T)
-    for t in range(max(rounds, ITERS)):
+    for t in range(max(rounds - 1, ITERS)):
         base = t * LANES
 
         def step(block, carry):
-            if t < rounds:
+            if t < rounds - 1:
                 eliminate(work, base, base, m - base, block)
             if t < ITERS:
                 eliminate(aug, 0, 0, r + m, block)
@@ -105,16 +109,6 @@
     basis_t = aug[:, pl.ds(r, m)]
     basis_ref[...] = basis_t
     factor_ref[...] = basis_t.T
-    row = lax.broadcasted_iota(jnp.int32, (LANES, LANES), 0)
-    col = lax.broadcasted_iota(jnp.int32, (LANES, LANES), 1)
-    for i in range(rounds):
-        for j in range(rounds):
-            spot = (pl.ds(j * LANES, LANES), pl.ds(i * LANES, LANES))
-            if j < i:
-                tri_ref[spot] = jnp.zeros((LANES, LANES), F32)
-                continue
-            piece = work[spot[::-1]]
-            tri_ref[spot] = (jnp.where(row <= col, piece, 0.0) if i == j else piece).T
 
 
 def solve(packed, start_block):
@@ -129,8 +123,11 @@
         ),
         in_specs=[vmem, vmem],
         out_specs=(vmem, vmem, vmem),
-        scratch_shapes=[pltpu.VMEM((m, m), F32), pltpu.VMEM((m, m), F32), pltpu.VMEM((r, r + m), F32)],
+        scratch_shapes=[pltpu.VMEM((m, m), F32), pltpu.VMEM((r, r + m), F32)],
         compiler_params=pltpu.CompilerParams(vmem_limit_bytes=32 * 1024 * 1024),
+        cost_estimate=pl.CostEstimate(
+            flops=12 * ITERS * r * m * (m + r) + 4 * m * m * m, bytes_accessed=8 * m * m, transcendentals=m
+        ),
         name="solve",
     )(packed, start_block)
 
@@ -261,7 +258,7 @@
     each = pl.cdiv(count, modes * rest * SUB) * SUB
     padded = each * modes * rest
     vmem = pl.BlockSpec(memory_space=pltpu.VMEM)
-    anywhere = pl.BlockSpec(memory_space=pl.ANY)
+    anywhere = pl.BlockSpec(memory_space=pltpu.HBM)
     most = max(cores, modes, depth)
     return pl.pallas_call(
         functools.partial(gram_kernel, (modes, cores, depth), cols_dev * rest),
@@ -284,19 +281,96 @@
             pltpu.SemaphoreType.DMA((CHUNKS,)),
         ],
         compiler_params=pltpu.CompilerParams(
-            collective_id=0, has_side_effects=True, vmem_limit_bytes=32 * 1024 * 1024
+            collective_id=0, has_side_effects=True, vmem_limit_bytes=61 * 1024 * 1024
         ),
         name="gram_sum",
     )(unfolded)
 
 
+def core_kernel(modes, basis_ref, full_ref, work_ref, tri_ref, core_ref, part, last, send, recv):
+    me_mode = lax.axis_index("mode")
+    me_rest = lax.axis_index("rest")
+    rows_dev = core_ref.shape[0]
+    width = full_ref.shape[1]
+    chunk = width // CHUNKS
+    others = [lax.rem(me_mode + off, modes) for off in range(1, modes)]
+    barrier = pltpu.get_barrier_semaphore()
+    for other in others:
+        pl.semaphore_signal(barrier, inc=1, device_id=(other, me_rest), device_id_type=MESH)
+    pl.semaphore_wait(barrier, modes - 1)
+    basis = basis_ref[...]
+    bh = basis.astype(BF16)
+    bl = (basis - bh.astype(F32)).astype(BF16)
+    copies = []
+    for c in range(CHUNKS):
+        cols = pl.ds(c * chunk, chunk)
+        x = full_ref[:, cols]
+        xh = x.astype(BF16)
+        xl = (x - xh.astype(F32)).astype(BF16)
+        part[:, cols] = nn(bh, xh) + (nn(bh, xl) + nn(bl, xh))
+        mine = pl.ds(pl.multiple_of(me_mode * width + c * chunk, chunk), chunk)
+        for at, other in enumerate(others):
+            copy = pltpu.make_async_remote_copy(
+                src_ref=part.at[pl.ds(pl.multiple_of(other * rows_dev, rows_dev), rows_dev), cols],
+                dst_ref=core_ref.at[:, mine],
+                send_sem=send.at[c, at],
+                recv_sem=recv.at[c, at],
+                device_id=(other, me_rest),
+                device_id_type=MESH,
+            )
+            copy.start()
+            copies.append(copy)
+        core_ref[:, mine] = part[pl.ds(pl.multiple_of(me_mode * rows_dev, rows_dev), rows_dev), cols]
+    rounds = work_ref.shape[0] // LANES
+    base = (rounds - 1) * LANES
+    last[...] = work_ref[pl.ds(base, LANES), pl.ds(base, LANES)]
+
+    def step(block, carry):
+        eliminate(last, 0, 0, LANES, block)
+        return carry
+
+    lax.fori_loop(0, LANES // STEP, step, 0)
+    row = lax.broadcasted_iota(jnp.int32, (LANES, LANES), 0)
+    col = lax.broadcasted_iota(jnp.int32, (LANES, LANES), 1)
+    for i in range(rounds):
+        for j in range(rounds):
+            spot = (pl.ds(j * LANES, LANES), pl.ds(i * LANES, LANES))
+            if j < i:
+                tri_ref[spot] = jnp.zeros((LANES, LANES), F32)
+                continue
+            piece = last[...] if i == rounds - 1 else work_ref[spot[::-1]]
+            tri_ref[spot] = (jnp.where(row <= col, piece, 0.0) if i == j else piece).T
+    for copy in copies:
+        copy.wait()
+
+
+def core_exchange(basis_t, full_rows, work, modes):
+    r = basis_t.shape[0]
+    m, width = full_rows.shape
+    vmem = pl.BlockSpec(memory_space=pltpu.VMEM)
+    return pl.pallas_call(
+        functools.partial(core_kernel, modes),
+        out_shape=(jax.ShapeDtypeStruct((m, m), F32), jax.ShapeDtypeStruct((r // modes, width * modes), F32)),
+        in_specs=[vmem, vmem, vmem],
+        out_specs=(vmem, vmem),
+        scratch_shapes=[
+            pltpu.VMEM((r, width), F32),
+            pltpu.VMEM((LANES, LANES), F32),
+            pltpu.SemaphoreType.DMA((CHUNKS, modes)),
+            pltpu.SemaphoreType.DMA((CHUNKS, modes)),
+        ],
+        compiler_params=pltpu.CompilerParams(
+            collective_id=1, has_side_effects=True, vmem_limit_bytes=32 * 1024 * 1024
+        ),
+        name="core_exchange",
+    )(basis_t, full_rows, work)
+
+
 def per_device(unfolded, start_block):
-    high = lax.Precision.HIGH
     modes, rest = lax.axis_size("mode"), lax.axis_size("rest")
     full_rows, packed = gram_sum(unfolded, modes, rest)
-    triangle, factor, basis_t = solve(packed, start_block)
-    partial_value = jnp.dot(basis_t, full_rows, precision=high)
-    core = lax.all_to_all(partial_value, "mode", split_axis=0, concat_axis=1, tiled=True)
+    work, factor, basis_t = solve(packed, start_block)
+    triangle, core = core_exchange(basis_t, full_rows, work, modes)
     return (triangle, factor, core)
 
 

time: 123 us -> 116 us (0.943)
  blocking collectives: 17.4 us -> 0 us
  Pallas kernels: 99.8 us -> 112 us
  matrix products: 1.49 us -> 0 us
    all_to_all x1 -> x0, blocking collectives: 17.4 us -> none  [per_device(): lax.all_to_all(partial_value, 'mode', split_axis=0, concat_axis=1, tiled=...]
    pallas_call x0 -> x1, Pallas kernels: none -> 15 us  [core_exchange(): pl.pallas_call(functools.partial(core_kernel, modes), out_shape=(jax.Shap...]
    pallas_call x1, Pallas kernels: 23.9 us -> 19.9 us  [solve(): pl.pallas_call(solve_kernel, out_shape=(jax.ShapeDtypeStruct((m, m), F32)...]
    dot_general x1 -> x0, matrix products: 1.49 us -> none  [per_device(): partial_value = jnp.dot(basis_t, full_rows, precision=high)]
    unnamed x4 -> x8, local copies, waits for them, and re-layouts: 2.18 us -> 3.18 us
where the time goes in v4:
time: 116 us; the launch traced here: 115 us
  Pallas kernels  112 us (97%)
  local copies, waits for them, and re-layouts  3.18 us (3%)
    pallas_call x1, Pallas kernels, gram_sum(): pl.pallas_call(functools.partial(gram_kernel, (modes, cores, depth), cols...  76.8 us
    pallas_call x1, Pallas kernels, solve(): pl.pallas_call(solve_kernel, out_shape=(jax.ShapeDtypeStruct((m, m), F32)...  19.9 us
    pallas_call x1, Pallas kernels, core_exchange(): pl.pallas_call(functools.partial(core_kernel, modes), out_shape=(jax.Shap...  15 us
    unnamed x8, local copies, waits for them, and re-layouts  3.18 us

profile of v4, /device:TPU:0, one launch (start us, length us, event | category | flops | bytes accessed | tf_op | source)
XLA Modules:
  0.0 115.5 jit_solution(8261985962707418322)
XLA Ops:
  0.6 0.0 copy-start.2
  0.6 76.8 %gram_sum.1 = (f32[512,2048]{1,0:T(8,128)}, f32[1280,128]{1,0:T(8,128)}) custom-call(f32[128,8192]{1,0:T(8,128)} %x_ref.1), custom_call_target="tpu_custom_call" | custom-call | tf_op jit(solution)/shard_map/gram_sum/pallas_call | solution.py:263
  77.4 0.0 copy-start
  77.4 0.0 copy-done.2
  77.4 0.0 copy-start.1
  77.4 1.2 %copy-done.1 = f32[1280,128]{1,0:T(8,128)S(1)} copy-done((f32[1280,128]{1,0:T(8,128)S(1)}, f32[1280,128]{1,0:T(8,128)}, u32[]{:S(2)}) %copy-start.1) | copy-done | bytes 655384
  78.7 19.9 %solve.1 = (f32[512,512]{1,0:T(8,128)S(1)}, f32[512,128]{1,0:T(8,128)}, f32[128,512]{1,0:T(8,128)S(1)}) custom-call(f32[1280,128]{1,0:T(8,128)S(1)} %copy-done.1, f32[512,128]{1,0:T(8,128)S(1)} %copy-done.2), custom_call_target="tpu_custom_call" | custom-call | flops 2046820352 | bytes 2097152 | tf_op jit(solution)/shard_map/solve/pallas_call | solution.py:117
  98.5 0.0 copy-done
  98.5 15.0 %core_exchange.1 = (f32[512,512]{1,0:T(8,128)S(1)}, f32[32,8192]{1,0:T(8,128)S(1)}) custom-call(f32[128,512]{1,0:T(8,128)S(1)} %get-tuple-element.11.basis_ref, f32[512,2048]{1,0:T(8,128)S(1)} %copy-done, f32[512,512]{1,0:T(8,128)S(1)} %get-tuple-element.13.work_ref), custom_call_target="tpu_custom_call" | custom-call | tf_op jit(solution)/shard_map/core_exchange/pallas_call | solution.py:351
  113.5 1.0 copy.7
  114.5 1.0 copy.8
Async XLA Ops:
  0.6 76.8 %copy-start.2 = (f32[512,128]{1,0:T(8,128)S(1)}, f32[512,128]{1,0:T(8,128)}, u32[]{:S(2)}) copy-start(f32[512,128]{1,0:T(8,128)} %start_ref.1) | copy-start | bytes 786436
  77.4 21.1 %copy-start = (f32[512,2048]{1,0:T(8,128)S(1)}, f32[512,2048]{1,0:T(8,128)}, u32[]{:S(2)}) copy-start(f32[512,2048]{1,0:T(8,128)} %get-tuple-element.12.full_ref) | copy-start | bytes 12582916
  77.4 1.2 %copy-start.1 = (f32[1280,128]{1,0:T(8,128)S(1)}, f32[1280,128]{1,0:T(8,128)}, u32[]{:S(2)}) copy-start(f32[1280,128]{1,0:T(8,128)} %get-tuple-element.10.packed_ref) | copy-start | bytes 1966084

commit v5 on v4

--- a/solution.py
+++ b/solution.py
@@ -10,7 +10,7 @@
 ITERS = 3
 SUB = 8
 STEP = 16
-CHUNKS = 4
+CHUNKS = 8
 LANES = 128
 F32 = jnp.float32
 BF16 = jnp.bfloat16

time: 116 us -> 116 us (level)
  no operation moved by 1% of the time
where the time goes in v5:
time: 116 us
  Pallas kernels  112 us (97%)
  local copies, waits for them, and re-layouts  3.18 us (3%)
    pallas_call x1, Pallas kernels, gram_sum(): pl.pallas_call(functools.partial(gram_kernel, (modes, cores, depth), cols...  76.4 us
    pallas_call x1, Pallas kernels, solve(): pl.pallas_call(solve_kernel, out_shape=(jax.ShapeDtypeStruct((m, m), F32)...  19.9 us
    pallas_call x1, Pallas kernels, core_exchange(): pl.pallas_call(functools.partial(core_kernel, modes), out_shape=(jax.Shap...  15.7 us
    unnamed x8, local copies, waits for them, and re-layouts  3.18 us

profile of v5, /device:TPU:0, one launch (start us, length us, event | category | flops | bytes accessed | tf_op | source)
XLA Modules:
  0.0 115.8 jit_solution(12941243248833300899)
XLA Ops:
  0.6 0.0 copy-start.2
  0.6 76.4 %gram_sum.1 = (f32[512,2048]{1,0:T(8,128)}, f32[1280,128]{1,0:T(8,128)}) custom-call(f32[128,8192]{1,0:T(8,128)} %x_ref.1), custom_call_target="tpu_custom_call" | custom-call | tf_op jit(solution)/shard_map/gram_sum/pallas_call | solution.py:263
  77.0 0.0 copy-start
  77.0 0.0 copy-done.2
  77.0 0.0 copy-start.1
  77.1 1.2 %copy-done.1 = f32[1280,128]{1,0:T(8,128)S(1)} copy-done((f32[1280,128]{1,0:T(8,128)S(1)}, f32[1280,128]{1,0:T(8,128)}, u32[]{:S(2)}) %copy-start.1) | copy-done | bytes 655384
  78.3 19.9 %solve.1 = (f32[512,512]{1,0:T(8,128)S(1)}, f32[512,128]{1,0:T(8,128)}, f32[128,512]{1,0:T(8,128)S(1)}) custom-call(f32[1280,128]{1,0:T(8,128)S(1)} %copy-done.1, f32[512,128]{1,0:T(8,128)S(1)} %copy-done.2), custom_call_target="tpu_custom_call" | custom-call | flops 2046820352 | bytes 2097152 | tf_op jit(solution)/shard_map/solve/pallas_call | solution.py:117
  98.2 0.0 copy-done
  98.2 15.7 %core_exchange.1 = (f32[512,512]{1,0:T(8,128)S(1)}, f32[32,8192]{1,0:T(8,128)S(1)}) custom-call(f32[128,512]{1,0:T(8,128)S(1)} %get-tuple-element.11.basis_ref, f32[512,2048]{1,0:T(8,128)S(1)} %copy-done, f32[512,512]{1,0:T(8,128)S(1)} %get-tuple-element.13.work_ref), custom_call_target="tpu_custom_call" | custom-call | tf_op jit(solution)/shard_map/core_exchange/pallas_call | solution.py:351
  113.8 1.0 copy.7
  114.8 1.0 copy.8
Async XLA Ops:
  0.6 76.4 %copy-start.2 = (f32[512,128]{1,0:T(8,128)S(1)}, f32[512,128]{1,0:T(8,128)}, u32[]{:S(2)}) copy-start(f32[512,128]{1,0:T(8,128)} %start_ref.1) | copy-start | bytes 786436
  77.0 21.1 %copy-start = (f32[512,2048]{1,0:T(8,128)S(1)}, f32[512,2048]{1,0:T(8,128)}, u32[]{:S(2)}) copy-start(f32[512,2048]{1,0:T(8,128)} %get-tuple-element.12.full_ref) | copy-start | bytes 12582916
  77.0 1.2 %copy-start.1 = (f32[1280,128]{1,0:T(8,128)S(1)}, f32[1280,128]{1,0:T(8,128)}, u32[]{:S(2)}) copy-start(f32[1280,128]{1,0:T(8,128)} %get-tuple-element.10.packed_ref) | copy-start | bytes 1966084
